TPU v7x, 512 devices: a whole 4x8x8 slice. The times are simulated.
512 devices in a mesh: member: 16 (over x, y_lo), space: 16 (over z, core), dp: 2 (over y_hi).
Axes of the slice: x: 4, y: 8 (y_hi: 2, y_lo: 4; y = y_hi * 4 + y_lo), z: 8, core: 2. Of those that a mesh axis runs over, the one named last changes fastest.
Arguments:
- latent: bfloat16 [16, 2, 16384, 1024], P('member', 'dp', 'space'), may hold values from -6 to 6
- target: bfloat16 [2, 100, 16384], P('dp', None, 'space'), may hold values from -6 to 6
- weight: bfloat16 [100, 1024], replicated, may hold values from -0.1875 to 0.1875
- bias: float32 [100], replicated, may hold values from -3 to 3
- gain: float32 [1024], replicated, may hold values from 0.1 to 1.9
- channel_weight: float32 [100], replicated, may hold values from 0.25 to 4
- band_offsets: int32 [17], replicated, may hold values from 0 to 80, as said below
- row_points: int32 [128], replicated, may hold values from 64 to 128, as said below
Outputs:
- grad_latent: bfloat16 [16, 2, 16384, 1024], P('member', 'dp', 'space')
- grad_weight: float32 [100, 1024], replicated
- grad_bias: float32 [100], replicated
- grad_gain: float32 [1024], replicated
- loss: float32 [], replicated
Inputs may be any that keep to these rules, and one draw needn't show every extreme that they name: `band_offsets`: nondecreasing, starting at 0; band s holds rows band_offsets[s] to band_offsets[s+1] - 1, at least 2 and at most 8 rows, and its points fill its first slots. `row_points`: the rows of one band hold at most 1024 points together, exactly 1024 in some band.
All inputs are finite; a program needn't handle non-finite values.
Results may differ from a plain program's by a relative error of at most 0.0084.
Values sent between devices are 32-bit elements; how exact they have to be, the bound alone decides.
A program may use at most 64 MiB of HBM per device.

v0:
```python
import jax
import jax.numpy as jnp
from jax import lax
from jax.sharding import PartitionSpec as P

smooth_sq = 0.01


def smooth_abs(value):
    return jnp.sqrt(value * value + smooth_sq)


def smooth_sign(value):
    return value / jnp.sqrt(value * value + smooth_sq)


def normalize(samples, gain):
    values = samples.astype(jnp.float32)
    middle = jnp.mean(values, axis=-1, keepdims=True)
    centered = values - middle
    variance = jnp.mean(centered * centered, axis=-1, keepdims=True)
    inverse = lax.rsqrt(variance + 1e-05)
    unit_rows = centered * inverse
    scaled = (unit_rows * gain).astype(jnp.bfloat16)
    return (unit_rows, inverse, scaled)


def shards(latent, target, weight, bias, gain, channel_weight, band_offsets, row_points):
    members = lax.axis_size("member")
    bands = lax.axis_size("space")
    band = lax.axis_index("space")
    own_member = lax.axis_index("member")
    row_ids = jnp.arange(row_points.shape[0], dtype=jnp.int32)
    in_band = (row_ids[None, :] >= band_offsets[:-1, None]) & (
        row_ids[None, :] < band_offsets[1:, None]
    )
    counts = jnp.sum(jnp.where(in_band, row_points[None, :], 0), axis=1)
    live_count = jnp.sum(jnp.where(jnp.arange(bands, dtype=jnp.int32) == band, counts, 0))
    total_live = jnp.sum(counts).astype(jnp.float32)
    samples = latent[0]
    slots = samples.shape[1]
    live = (jnp.arange(slots, dtype=jnp.int32) < live_count).astype(jnp.float32)
    unit_rows, inverse, scaled = normalize(samples, gain)
    predicted = (
        jnp.einsum("bph,ch->bcp", scaled, weight, preferred_element_type=jnp.float32)
        + bias[None, :, None]
    )
    grid_weight = channel_weight[None, :, None] * live[None, None, :]
    error = predicted - target.astype(jnp.float32)
    skill = jnp.sum(grid_weight * smooth_abs(error))
    pair_weight = 1.0 / (members - 1)
    piece = lax.all_gather(predicted[None], "member", axis=0, tiled=True)
    count = piece.shape[0]
    others = (jnp.arange(count, dtype=jnp.int32) != own_member).astype(jnp.float32)[
        :, None, None, None
    ]
    spread_gap = predicted[None] - piece
    spread_sum = jnp.sum(grid_weight[None] * others * smooth_abs(spread_gap))
    slope_sum = jnp.sum(others * smooth_sign(spread_gap), axis=0)
    local_score = skill - 0.5 * pair_weight * spread_sum
    dpred = grid_weight * (smooth_sign(error) - pair_weight * slope_sum)
    dpred_low = dpred.astype(jnp.bfloat16)
    grad_w = jnp.einsum("bcp,bph->ch", dpred_low, scaled, preferred_element_type=jnp.float32)
    grad_b = jnp.sum(dpred, axis=(0, 2))
    dscaled = jnp.einsum("bcp,ch->bph", dpred_low, weight, preferred_element_type=jnp.float32)
    grad_g = jnp.sum(dscaled * unit_rows, axis=(0, 1))
    dunit = dscaled * gain
    first = jnp.mean(dunit, axis=-1, keepdims=True)
    second = jnp.mean(dunit * unit_rows, axis=-1, keepdims=True)
    grad_x = (inverse * (dunit - first - unit_rows * second)).astype(jnp.bfloat16)
    sum_w, sum_b, sum_g, sum_score = lax.psum(
        (grad_w, grad_b, grad_g, local_score), ("member", "space", "dp")
    )
    batch = samples.shape[0] * lax.axis_size("dp")
    loss = sum_score / (weight.shape[0] * batch * total_live)
    return (grad_x[None], sum_w, sum_b, sum_g, loss)


def solution(mesh):
    return jax.shard_map(
        shards,
        mesh=mesh,
        in_specs=(
            P("member", "dp", "space", None),
            P("dp", None, "space"),
            P(),
            P(),
            P(),
            P(),
            P(),
            P(),
        ),
        out_specs=(P("member", "dp", "space", None), P(), P(), P(), P()),
        check_vma=False,
    )
```

profile of v0, /device:TPU:1, one launch (start us, length us, event | category | flops | bytes accessed | tf_op | source)
XLA Modules:
  0.0 467.6 jit_solution(11264365382467686688)
XLA Ops:
  7.2 0.0 copy-start
  7.2 0.0 copy-start.3
  7.2 0.0 copy-start.7
  7.2 0.0 all-gather.4.cloned.1.call-start
  7.2 2.9 copy.17
  10.2 0.4 convert_reduce_fusion
  10.5 0.0 copy-start.6
  10.6 0.0 copy-start.4
  10.6 0.6 fusion.2
  11.2 0.0 copy-done
  11.2 1.6 fusion.30
  12.8 0.0 all-gather.4.cloned.1.call-update
  12.8 0.0 all-reduce.3.cloned.1.call-start
  12.9 0.1 fusion.43
  13.0 0.7 select_reduce_fusion
  14.3 0.6 fusion.41
  15.0 0.6 fusion.40
  15.6 0.0 copy-done.4
  15.6 0.0 copy-start.1
  15.6 0.0 copy-start.2
  15.6 0.1 broadcast_multiply_fusion
  15.8 159.0 %all-gather.4.cloned.1.call-done = f32[16,100,1024]{2,1,0:T(8,128)} async-done(((f32[1,100,1024]{2,1,0:T(8,128)}), f32[16,100,1024]{2,1,0:T(8,128)}) %all-gather.4.cloned.1.call-update) | async-done | bytes 6553616 | tf_op jit(solution)/shard_map/all_gather | solution.py:52
  174.8 6.8 %multiply_reduce_fusion = (f32[]{:T(128)}, f32[100,1024]{1,0:T(8,128)S(1)}) fusion(f32[16,100,1024]{2,1,0:T(8,128)} %all-gather.4.cloned.1.call-done, f32[100,1024]{1,0:T(8,128)S(1)} %broadcast_multiply_fusion, f32[100,1024]{1,0:T(8,128)} %bitcast.71, f32[16]{0:T(128)S(1)} %compare_convert_fusion), kind=kLoop, calls=%fused_computation.5 | loop fusion | flops 14643199 | bytes 7782468 | tf_op jit(solution)/shard_map/reduce_sum | solution.py:58
  181.5 1.0 fusion.42
  182.5 1.6 fusion.22
  184.2 3.4 fusion.17
  187.6 0.0 all-reduce.3.cloned.1.call-update
  187.6 4.7 %fusion.18 = bf16[1,1,1024,1024]{2,3,1,0:T(8,128)(2,1)} fusion(bf16[1,1,1024,1024]{2,3,1,0:T(8,128)(2,1)S(1)} %copy.17, f32[1024,1024]{0,1:T(8,128)} %get-tuple-element.35, f32[1024]{0:T(1024)S(1)} %get-tuple-element.36, f32[1024]{0:T(1024)S(1)} %get-tuple-element.37, f32[1024]{0:T(1024)S(1)} %copy-done.3, f32[1024]{0:T(1024)S(1)} %broadcast_multiply_fusion.3, ...), kind=kLoop, calls=%fused_computation.27 | loop fusion | flops 9437184 | bytes 8409088 | tf_op jit(solution)/shard_map/broadcast_in_dim | solution.py:76
  192.3 3.9 copy.18
  197.6 99.5 %all-reduce = (f32[100]{0:T(128)}, f32[1024]{0:T(1024)}, f32[]{:T(128)}) all-reduce(f32[100]{0:T(128)S(1)} %get-tuple-element.30, f32[1024]{0:T(1024)S(1)} %get-tuple-element.22, f32[]{:T(128)S(6)} %sub.72), channel_id=1, replica_groups=mesh['member'=16,'space'=16,'dp'=2] {'member','space','dp'}, use_global_device_ids=true, to_apply=%region_9.10 | all-reduce | flops 1125 | bytes 9000 | tf_op jit(solution)/shard_map/psum | solution.py:71
  297.7 160.1 %all-reduce.3.cloned.1.call-done = f32[100,1024]{1,0:T(8,128)} async-done(((f32[100,1024]{1,0:T(8,128)}), f32[100,1024]{1,0:T(8,128)}) %all-reduce.3.cloned.1.call-update) | async-done | bytes 409616 | tf_op jit(solution)/shard_map/psum | solution.py:71
  457.8 1.8 copy.20
  (11 shorter events, 0.0 us)
Async XLA Ops:
  7.2 4.0 copy-start
  7.2 4.0 copy-start.3
  7.2 4.0 copy-start.7
  7.2 167.6 %all-gather.4.cloned.1.call-start = ((), (), s32[]{:S(2)}) async-start(), calls=%async_computation.1 | async-start | bytes 7241728 | tf_op jit(solution)/shard_map/all_gather | solution.py:52
  10.5 2.3 copy-start.5
  10.5 2.4 copy-start.6
  10.6 5.1 %copy-start.4 = (f32[100]{0:T(128)S(1)}, f32[100]{0:T(128)}, u32[]{:S(2)}) copy-start(f32[100]{0:T(128)} %param.13) | copy-start | bytes 1204
  12.8 445.0 %all-reduce.3.cloned.1.call-start = ((), (), s32[]{:S(2)}) async-start(), calls=%async_computation | async-start | bytes 851968 | tf_op jit(solution)/shard_map/psum | solution.py:71
  15.6 165.9 %copy-start.1 = (f32[1024,100]{0,1:T(8,128)S(1)}, f32[1024,100]{0,1:T(8,128)}, u32[]{:S(2)}) copy-start(f32[1024,100]{0,1:T(8,128)} %fusion.30) | copy-start | bytes 1228804
  15.6 165.9 %copy-start.2 = (bf16[1,100,1024]{2,1,0:T(8,128)(2,1)S(1)}, bf16[1,100,1024]{2,1,0:T(8,128)(2,1)}, u32[]{:S(2)}) copy-start(bf16[1,100,1024]{2,1,0:T(8,128)(2,1)} %param.9) | copy-start | bytes 614404
Sparse Core Ops, SparseCore 0:
  12.9 161.7 all-gather.3
  187.7 270.0 all-reduce.2
where the time goes:
time: 468 us
  waiting for transfers between devices  319 us (68%)
  blocking collectives  99.5 us (21%)
  between operations  17.9 us (4%)
  other arithmetic  15.5 us (3%)
  local copies, waits for them, and re-layouts  8.76 us (2%)
  matrix products  6.64 us (1%)
    psum x1, waiting for transfers between devices, shards(): lax.psum((grad_w, grad_b, grad_g, local_score), ('member', 'space', 'dp'))  160 us
    all_gather x1, waiting for transfers between devices, shards(): piece = lax.all_gather(predicted[None], 'member', axis=0, tiled=True)  159 us
    psum x1, blocking collectives, shards(): lax.psum((grad_w, grad_b, grad_g, local_score), ('member', 'space', 'dp'))  99.5 us
  transfers between devices with their start and end apart: 2, of which 2 were waited for; matrix products, arithmetic and copies ran while one was open for 2% of the time, Pallas kernels for 0%

commit v1 on v0

--- a/solution.py
+++ b/solution.py
@@ -49,7 +49,10 @@
     error = predicted - target.astype(jnp.float32)
     skill = jnp.sum(grid_weight * smooth_abs(error))
     pair_weight = 1.0 / (members - 1)
-    piece = lax.all_gather(predicted[None], "member", axis=0, tiled=True)
+    piece = jnp.concatenate(
+        lax.all_to_all(jnp.stack([predicted[None]] * lax.axis_size("member")), "member", 0, 0),
+        axis=0,
+    )
     count = piece.shape[0]
     others = (jnp.arange(count, dtype=jnp.int32) != own_member).astype(jnp.float32)[
         :, None, None, None

time: 468 us -> 503 us (1.075)
  other arithmetic: 15.5 us -> 49.7 us
  waiting for transfers between devices: 319 us -> 302 us
  starting transfers between devices: 0.08 us -> 8.21 us
  local copies, waits for them, and re-layouts: 8.76 us -> 15.1 us
    all_gather x1 -> x0, waiting for transfers between devices: 159 us -> none  [shards(): piece = lax.all_gather(predicted[None], 'member', axis=0, tiled=True)]
    all_to_all x0 -> x1, waiting for transfers between devices: none -> 143 us  [shards(): lax.all_to_all(jnp.stack([predicted[None]] * lax.axis_size('member')), 'm...]
    reduce_sum x1, other arithmetic: 6.77 us -> 40.9 us  [shards(): spread_sum = jnp.sum(grid_weight[None] * others * smooth_abs(spread_gap))]
    all_to_all x0 -> x1, starting transfers between devices: none -> 8.17 us  [shards(): lax.all_to_all(jnp.stack([predicted[None]] * lax.axis_size('member')), 'm...]
    another operation x0 -> x1, local copies, waits for them, and re-layouts: none -> 6.33 us  [shards(): jnp.stack([predicted[None]] * lax.axis_size('member'))]
where the time goes in v1:
time: 503 us
  waiting for transfers between devices  302 us (60%)
  blocking collectives  104 us (21%)
  other arithmetic  49.7 us (10%)
  between operations  17.9 us (4%)
  local copies, waits for them, and re-layouts  15.1 us (3%)
  starting transfers between devices  8.21 us (2%)
  matrix products  5.88 us (1%)
    psum x1, waiting for transfers between devices, shards(): lax.psum((grad_w, grad_b, grad_g, local_score), ('member', 'space', 'dp'))  159 us
    all_to_all x1, waiting for transfers between devices, shards(): lax.all_to_all(jnp.stack([predicted[None]] * lax.axis_size('member')), 'm...  143 us
    psum x1, blocking collectives, shards(): lax.psum((grad_w, grad_b, grad_g, local_score), ('member', 'space', 'dp'))  104 us
    reduce_sum x1, other arithmetic, shards(): spread_sum = jnp.sum(grid_weight[None] * others * smooth_abs(spread_gap))  40.9 us
  transfers between devices with their start and end apart: 2, of which 2 were waited for; matrix products, arithmetic and copies ran while one was open for 2% of the time, Pallas kernels for 0%

profile of v1, /device:TPU:1, one launch (start us, length us, event | category | flops | bytes accessed | tf_op | source)
XLA Modules:
  0.0 502.8 jit_solution(10419337186003777410)
XLA Ops:
  7.2 0.0 copy-start
  7.2 0.0 copy-start.6
  7.2 0.0 copy-start.2
  7.2 2.9 copy.17
  10.1 0.4 convert_reduce_fusion
  10.5 0.6 fusion.2
  11.1 0.0 copy-done
  11.1 0.0 copy-done.6
  11.1 0.0 copy-done.2
  11.1 0.8 fusion.30
  12.0 6.3 %stack.3 = f32[16,1,1,100,1024]{4,2,3,1,0:T(1,128)} broadcast(f32[100,1024]{1,0:T(8,128)S(1)} %bitcast.73), dimensions={3,4} | broadcast | bytes 6963200 | tf_op jit(solution)/shard_map/stack | solution.py:53
  18.3 8.2 %all-to-all-start = ((f32[16,1,1,100,1024]{4,2,3,1,0:T(1,128)}), f32[16,1,1,100,1024]{4,2,3,1,0:T(1,128)}, u32[]{:S(2)}, u32[]{:S(2)}) async-start(f32[16,1,1,100,1024]{4,2,3,1,0:T(1,128)} %stack.3), calls=%async_computation | async-start | bytes 13107200 | tf_op jit(solution)/shard_map/all_to_all | solution.py:53
  26.5 0.0 copy-start.1
  26.5 0.0 all-reduce.3.cloned.1.call-start
  26.6 0.1 fusion.43
  26.6 0.0 copy-done.5
  26.6 0.7 select_reduce_fusion
  28.0 0.6 fusion.41
  28.6 0.6 fusion.40
  29.3 0.1 broadcast_multiply_fusion
  29.4 143.0 %all-to-all-done = f32[16,1,1,100,1024]{4,2,3,1,0:T(1,128)} async-done(((f32[16,1,1,100,1024]{4,2,3,1,0:T(1,128)}), f32[16,1,1,100,1024]{4,2,3,1,0:T(1,128)}, u32[]{:S(2)}, u32[]{:S(2)}) %all-to-all-start) | async-done | bytes 6553632 | tf_op jit(solution)/shard_map/all_to_all | solution.py:53
  172.4 40.9 %multiply_reduce_fusion = (f32[]{:T(128)}, f32[100,1024]{1,0:T(8,128)S(1)}) fusion(f32[16,1,1,100,1024]{4,2,3,1,0:T(1,128)} %all-to-all-done, f32[100,1024]{1,0:T(8,128)S(1)} %broadcast_multiply_fusion, f32[100,1024]{1,0:T(8,128)S(1)} %bitcast.74, f32[16]{0:T(128)S(1)} %compare_convert_fusion), kind=kLoop, calls=%fused_computation.5 | loop fusion | flops 14643199 | bytes 7782468 | tf_op jit(solution)/shard_map/reduce_sum | solution.py:61
  213.3 0.0 copy-done.1
  213.3 1.0 fusion.42
  214.3 3.4 fusion.17
  217.7 1.7 fusion.22
  219.3 0.0 all-reduce.3.cloned.1.call-update
  219.4 4.7 fusion.18
  224.1 3.9 copy.18
  229.3 103.6 %all-reduce = (f32[100]{0:T(128)}, f32[1024]{0:T(1024)}, f32[]{:T(128)}) all-reduce(f32[100]{0:T(128)S(1)} %get-tuple-element.30, f32[1024]{0:T(1024)S(1)} %get-tuple-element.22, f32[]{:T(128)S(6)} %sub.84), channel_id=1, replica_groups=mesh['member'=16,'space'=16,'dp'=2] {'member','space','dp'}, use_global_device_ids=true, to_apply=%region_9.10 | all-reduce | flops 1125 | bytes 9000 | tf_op jit(solution)/shard_map/psum | solution.py:74
  333.6 159.4 %all-reduce.3.cloned.1.call-done = f32[100,1024]{1,0:T(8,128)} async-done(((f32[100,1024]{1,0:T(8,128)}), f32[100,1024]{1,0:T(8,128)}) %all-reduce.3.cloned.1.call-update) | async-done | bytes 409616 | tf_op jit(solution)/shard_map/psum | solution.py:74
  493.0 1.8 copy.20
  (9 shorter events, 0.0 us)
Async XLA Ops:
  7.2 4.0 copy-start
  7.2 3.9 copy-start.6
  7.2 3.9 copy-start.2
  18.3 8.3 %copy-start.4 = (s32[17]{0:T(128)S(1)}, s32[17]{0:T(128)}, u32[]{:S(2)}) copy-start(s32[17]{0:T(128)} %param.14) | copy-start | bytes 208
  18.3 8.3 %copy-start.5 = (s32[128]{0:T(128)S(1)}, s32[128]{0:T(128)}, u32[]{:S(2)}) copy-start(s32[128]{0:T(128)} %param.15) | copy-start | bytes 1540
  18.3 11.0 %copy-start.3 = (f32[100]{0:T(128)S(1)}, f32[100]{0:T(128)}, u32[]{:S(2)}) copy-start(f32[100]{0:T(128)} %param.13) | copy-start | bytes 1204
  18.3 154.1 %all-to-all-start = ((f32[16,1,1,100,1024]{4,2,3,1,0:T(1,128)}), f32[16,1,1,100,1024]{4,2,3,1,0:T(1,128)}, u32[]{:S(2)}, u32[]{:S(2)}) async-start(f32[16,1,1,100,1024]{4,2,3,1,0:T(1,128)} %stack.3), calls=%async_computation | async-start | bytes 13107200 | tf_op jit(solution)/shard_map/all_to_all | solution.py:53
  26.5 186.8 %copy-start.1 = (bf16[1,100,1024]{2,1,0:T(8,128)(2,1)S(1)}, bf16[1,100,1024]{2,1,0:T(8,128)(2,1)}, u32[]{:S(2)}) copy-start(bf16[1,100,1024]{2,1,0:T(8,128)(2,1)} %param.9) | copy-start | bytes 614404
  26.5 466.5 %all-reduce.3.cloned.1.call-start = ((), (), s32[]{:S(2)}) async-start(), calls=%async_computation.1 | async-start | bytes 851968 | tf_op jit(solution)/shard_map/psum | solution.py:74
Sparse Core Ops, SparseCore 0:
  219.5 273.5 all-reduce.2
